TPU v7x, 512 devices: a whole 4x8x8 slice. The times are simulated.
512 devices in a mesh: scalp: 256 (over z, y, x), screen: 2 (over core).
Axes of the slice: x: 4, y: 8, z: 8, core: 2. Of those that a mesh axis runs over, the one named last changes fastest.
Arguments:
- guides: bfloat16 [1048576, 384], P('scalp'), may hold values from -6 to 6
- neighbours: int32 [2048, 32], P(('scalp', 'screen')), may hold values from 0 to 1048575, as said below
- pick: int32 [2048, 4, 256], P(('scalp', 'screen')), may hold values from 0 to 31, as said below
- pick_weight: bfloat16 [2048, 4, 256], P(('scalp', 'screen')), may hold values from 0.099609375 to 0.59765625
- keep: int32 [2048, 256], P(('scalp', 'screen')), may hold values 0 or 1
- width: float32 [2048, 256], P(('scalp', 'screen')), may hold values from 0.2 to 2
- route: int32 [2048, 1], P(('scalp', 'screen')), may hold values from 0 to 1; in each aligned block of 4 rows (0 to 3, 4 to 7, ...) at most 3 rows name the same one
- tess_centre: bfloat16 [2, 384, 768], P('screen'), may hold values from -0.3125 to 0.3125
- tess_side: bfloat16 [2, 384, 768], P('screen'), may hold values from -0.3125 to 0.3125
Outputs:
- ribbon: bfloat16 [786432, 768], P(('scalp', 'screen'))
Inputs may be any that keep to these rules, and one draw needn't show every extreme that they name: `neighbours`: each entry names a guide of the render block's own scalp tile or of the scalp tile just before or after it, wrapping around; a block of device (s, c) belongs to scalp tile s. `pick`: the 4 entries of one render strand differ. `route`: among the 4 blocks of one device at most 3 name the same screen tile.
All inputs are finite; a program needn't handle non-finite values. No bound on the sum of `keep` on one device may be relied on, other than what follows from the above.
Results may differ from a plain program's by a relative error of at most 0.009.
Values may be sent and summed in bfloat16 or wider, within the bound.
No kernel may reach another device: no remote copies, remote signals or barrier semaphores. Data moves between devices by JAX's collectives and lax.ppermute only.
A program may use at most 64 MiB of HBM per device.

v0:
```python
import functools

import jax
import jax.numpy as jnp
from jax import lax
from jax.experimental import pallas as pl
from jax.experimental.pallas import tpu as pltpu
from jax.sharding import PartitionSpec as P


F32 = jnp.float32
BF16 = jnp.bfloat16
VMEM = pl.BlockSpec(memory_space=pltpu.VMEM)
HBM = pl.BlockSpec(memory_space=pltpu.HBM)
SMEM = pl.BlockSpec(memory_space=pltpu.SMEM)
CHUNK = 256
LIMIT = 16 * 1024 * 1024


def iota(shape, dim):
    return lax.broadcasted_iota(jnp.int32, shape, dim)


def fill_hot(hot_ref, index, valid):
    rows = index.shape[0]
    high = jnp.floor(index * (1.0 / CHUNK))
    low = index - high * CHUNK
    low = low if valid is None else jnp.where(valid, low, -1.0)
    lanes = iota((rows, CHUNK), 1).astype(F32)
    for part in range(hot_ref.shape[1] // CHUNK):
        key = jnp.where(high == part, low, -1.0)
        hot_ref[:, part * CHUNK : (part + 1) * CHUNK] = jnp.where(key == lanes, 1.0, 0.0).astype(BF16)


def serve_kernel(first_ref, second_ref, table_ref, out_ref, hot_ref):
    listed = first_ref.shape[1]
    tile = table_ref.shape[0]
    ask = jnp.concatenate([first_ref[...], second_ref[...]], axis=0)
    blocks = ask.shape[0]
    within = jnp.bitwise_and(ask, tile - 1).astype(F32)
    wide = jnp.concatenate(
        [jnp.broadcast_to(within[b : b + 1, :], (listed, listed)) for b in range(blocks)], axis=0
    )
    on = jnp.bitwise_and(iota(wide.shape, 0), listed - 1) == iota(wide.shape, 1)
    index = jnp.sum(jnp.where(on, wide, 0.0), axis=1, keepdims=True)
    fill_hot(hot_ref, index, None)
    out_ref[...] = jnp.dot(hot_ref[...], table_ref[...], preferred_element_type=F32).astype(BF16)


def mark_kernel(out_ref):
    out_ref[...] = jnp.zeros_like(out_ref)


def pack_kernel(mark_ref, route_ref, *refs):
    del mark_ref
    *refs, out_ref = refs
    neighbours_ref, pick_ref, weight_ref, keep_ref, width_ref = refs
    blocks, picks, strands = pick_ref.shape
    times = strands // neighbours_ref.shape[1]
    for b in range(blocks):
        tile = route_ref[b]
        rank = jnp.int32(0)
        for e in range(b):
            rank = rank + jnp.where(route_ref[e] == tile, 1, 0)
        kept = keep_ref[b : b + 1, :].astype(F32)
        scaled = width_ref[b : b + 1, :] * strands / (jnp.sum(kept, axis=1, keepdims=True) + 1.0)
        out_ref[b, 0:picks, :] = pick_ref[b].astype(F32)
        out_ref[b, picks : 2 * picks, :] = weight_ref[b].astype(F32)
        out_ref[b, 8:9, :] = kept
        out_ref[b, 9:10, :] = kept * scaled
        out_ref[b, 10:11, :] = jnp.full((1, strands), tile.astype(F32))
        out_ref[b, 11:12, :] = jnp.full((1, strands), rank.astype(F32))
        listed = neighbours_ref[b : b + 1, :].astype(F32)
        out_ref[b, 12:13, :] = jnp.concatenate([listed] * times, axis=1)
        out_ref[b, 13:16, :] = jnp.zeros((3, strands), F32)


def plan_kernel(mine_ref, theirs_ref, table_ref, own_ref, sel_r_ref, sel_x_ref, mix_ref, hot_ref, *, scalps, slots):
    half = mine_ref.shape[0]
    blocks = 2 * half
    listed = mix_ref.shape[2] // 2
    tile = table_ref.shape[0]
    core = lax.axis_index("screen")
    here = lax.axis_index("scalp")
    strands = mine_ref.shape[2]
    lanes = blocks * listed
    core_f = core.astype(F32)
    codes = []
    for group, ref in enumerate((mine_ref, theirs_ref)):
        for b in range(half):
            goes = ref[b, 10:11, :] == core_f
            codes.append(jnp.where(goes, ref[b, 11:12, :], -1.0))
        for q in range(slots):
            packed = jnp.zeros((16, strands), F32)
            for b in range(half):
                packed = packed + jnp.where(codes[group * half + b] == q, ref[b], 0.0)
            spread = jnp.zeros((listed, strands), F32)
            row = iota((listed, strands), 0).astype(F32)
            for j in range(4):
                spread = spread + jnp.where(row == packed[j : j + 1, :], packed[4 + j : 5 + j, :], 0.0)
            both = jnp.concatenate([spread * packed[8:9, :], spread * packed[9:10, :]], axis=0)
            mix_ref[group * slots + q] = both.T.astype(BF16)
    block_of = iota((1, lanes), 1) // listed
    code = jnp.zeros((1, lanes), F32)
    ask = jnp.zeros((1, lanes), F32)
    for b in range(blocks):
        ref = (mine_ref, theirs_ref)[b // half]
        code = code + jnp.where(block_of == b, codes[b][:, :lanes], 0.0)
        ask = ask + jnp.where(block_of == b, ref[b % half, 12:13, :lanes], 0.0)
    owner = jnp.floor(ask * (1.0 / tile))
    within = ask - owner * tile
    relative = owner - here.astype(F32) + 1.0
    relative = jnp.where(relative < 0.0, relative + scalps, relative)
    relative = jnp.where(relative >= scalps, relative - scalps, relative)
    rows = 2 * slots * listed
    r = iota((rows, lanes), 0)
    l = iota((rows, lanes), 1)
    base = (r % listed == l % listed) & (r // (slots * listed) == l // (half * listed))
    base = base & (((r // listed) % slots).astype(F32) == code)
    near = 2.0 - 2.0 * core_f
    sel_r = jnp.where(base & (relative == near), 1.0, 0.0)
    sel_x = jnp.where(base & (relative == 2.0 - near), 1.0, 0.0)
    sel_o = jnp.where(base & (relative == 1.0), 1.0, 0.0)
    sel_r_ref[...] = sel_r.astype(BF16)
    swap = half * listed
    sel_x_ref[...] = jnp.concatenate([sel_x[:, swap:], sel_x[:, :swap]], axis=1).astype(BF16)
    index = jnp.sum(sel_o * within, axis=1, keepdims=True)
    valid = jnp.sum(sel_o, axis=1, keepdims=True) > 0.5
    fill_hot(hot_ref, index, valid)
    own_ref[...] = jnp.dot(hot_ref[...], table_ref[...], preferred_element_type=F32).astype(BF16)


def ribbon_kernel(near_ref, far_ref, own_ref, sel_r_ref, sel_x_ref, mix_ref, centre_ref, side_ref, out_ref, buffer, sems):
    total, strands, depth = mix_ref.shape
    listed = depth // 2
    slots = total // 2
    core = lax.axis_index("screen")
    rows = jnp.dot(sel_r_ref[...], near_ref[...], preferred_element_type=F32)
    rows = rows + jnp.dot(sel_x_ref[...], far_ref[...], preferred_element_type=F32)
    rows = (rows + own_ref[...].astype(F32)).astype(BF16)
    centre = jnp.dot(rows, centre_ref[0], preferred_element_type=F32).astype(BF16)
    side = jnp.dot(rows, side_ref[0], preferred_element_type=F32).astype(BF16)
    copies = []
    for i in range(total):
        both = jnp.concatenate(
            [centre[i * listed : (i + 1) * listed], side[i * listed : (i + 1) * listed]], axis=0
        )
        buffer[i] = jnp.dot(mix_ref[i], both, preferred_element_type=F32).astype(BF16)
        device = core if i < slots else 1 - core
        place = device * slots + i % slots
        copy = pltpu.make_async_copy(
            buffer.at[i], out_ref.at[pl.ds(pl.multiple_of(place * strands, strands), strands)], sems.at[i]
        )
        copy.start()
        copies.append(copy)
    for copy in copies:
        copy.wait()


def cost(flops, bytes_accessed):
    return pl.CostEstimate(flops=flops, bytes_accessed=bytes_accessed, transcendentals=0)


def body(guides, neighbours, pick, pick_weight, keep, width, route, tess_centre, tess_side):
    scalps = lax.axis_size("scalp")
    screens = lax.axis_size("screen")
    tile, depth = guides.shape
    blocks, listed = neighbours.shape
    strands = keep.shape[1]
    slots = blocks // screens + blocks // 4
    points = tess_centre.shape[2]
    swap = [(0, 1), (1, 0)]
    both = ("scalp", "screen")
    ask_pairs, cross_pairs = [], []
    for s in range(scalps):
        high, low = 2 * ((s + 1) % scalps), 2 * ((s - 1) % scalps) + 1
        ask_pairs += [(2 * s, high), (2 * s + 1, low)]
        cross_pairs += [(2 * s + 1, high), (2 * s, low)]
    reply_pairs = [(b, a) for a, b in ask_pairs]
    pass_pairs = [(b, a) for a, b in cross_pairs]

    mark = pl.pallas_call(
        mark_kernel,
        out_shape=jax.ShapeDtypeStruct((8, 128), F32),
        out_specs=VMEM,
        cost_estimate=cost(20_000_000_000, 2_000_000),
        compiler_params=pltpu.CompilerParams(vmem_limit_bytes=LIMIT),
        name="mark",
    )()
    first = lax.ppermute(neighbours, both, ask_pairs)
    second = lax.ppermute(neighbours, both, cross_pairs)
    parts = (neighbours, pick, pick_weight, keep, width)
    packed = pl.pallas_call(
        pack_kernel,
        out_shape=jax.ShapeDtypeStruct((blocks, 16, strands), F32),
        in_specs=[VMEM, SMEM] + [VMEM] * len(parts),
        out_specs=VMEM,
        cost_estimate=cost(blocks * 16 * strands, blocks * 32 * strands),
        compiler_params=pltpu.CompilerParams(vmem_limit_bytes=LIMIT),
        name="pack",
    )(mark, route[:, 0], *parts)
    first, packed = lax.optimization_barrier((first, packed))
    all_rows = 2 * blocks * listed
    served = pl.pallas_call(
        serve_kernel,
        out_shape=jax.ShapeDtypeStruct((all_rows, depth), BF16),
        in_specs=[VMEM, VMEM, VMEM],
        out_specs=VMEM,
        scratch_shapes=[pltpu.VMEM((all_rows, tile), BF16)],
        cost_estimate=cost(2 * all_rows * tile * depth, tile * depth * 2),
        compiler_params=pltpu.CompilerParams(vmem_limit_bytes=LIMIT),
        name="serve",
    )(first, second, guides)
    served, packed = lax.optimization_barrier((served, packed))
    near = lax.ppermute(served, both, reply_pairs)
    far = lax.ppermute(served, both, pass_pairs)
    theirs = lax.ppermute(packed, "screen", swap)
    total = 2 * slots
    own, sel_r, sel_x, mix = pl.pallas_call(
        functools.partial(plan_kernel, scalps=scalps, slots=slots),
        out_shape=(
            jax.ShapeDtypeStruct((total * listed, depth), BF16),
            jax.ShapeDtypeStruct((total * listed, all_rows), BF16),
            jax.ShapeDtypeStruct((total * listed, all_rows), BF16),
            jax.ShapeDtypeStruct((total, strands, 2 * listed), BF16),
        ),
        in_specs=[VMEM, VMEM, VMEM],
        out_specs=(VMEM, VMEM, VMEM, VMEM),
        scratch_shapes=[pltpu.VMEM((total * listed, tile), BF16)],
        cost_estimate=cost(2 * total * listed * tile * depth, tile * depth * 2),
        compiler_params=pltpu.CompilerParams(vmem_limit_bytes=LIMIT),
        name="plan",
    )(packed, theirs, guides)
    return pl.pallas_call(
        ribbon_kernel,
        out_shape=jax.ShapeDtypeStruct((total * strands, points), BF16),
        in_specs=[VMEM] * 8,
        out_specs=pl.BlockSpec(memory_space=pl.ANY),
        scratch_shapes=[pltpu.VMEM((total, strands, points), BF16), pltpu.SemaphoreType.DMA((total,))],
        cost_estimate=cost(2 * total * strands * points * 256, total * strands * points * 2),
        compiler_params=pltpu.CompilerParams(vmem_limit_bytes=LIMIT),
        name="ribbon",
    )(near, far, own, sel_r, sel_x, mix, tess_centre, tess_side)


def solution(mesh):
    return jax.shard_map(
        body,
        mesh=mesh,
        in_specs=(
            P("scalp", None),
            P(("scalp", "screen"), None),
            P(("scalp", "screen"), None, None),
            P(("scalp", "screen"), None, None),
            P(("scalp", "screen"), None),
            P(("scalp", "screen"), None),
            P(("scalp", "screen"), None),
            P("screen", None, None),
            P("screen", None, None),
        ),
        out_specs=P(("scalp", "screen"), None),
        check_vma=False,
    )
```

profile of v0, /device:TPU:1, one launch (start us, length us, event | category | flops | bytes accessed | tf_op | source)
XLA Modules:
  0.0 39.8 jit_solution(1220770795539010875)
XLA Ops:
  0.0 0.0 copy-start.7
  0.0 0.0 copy-start.8
  0.0 0.0 copy-start.6
  0.0 0.0 copy-start.5
  0.0 0.0 copy-start.4
  0.0 0.0 copy-start.3
  0.0 0.0 copy-start
  0.0 16.8 %collective-permute-start = (s32[4,32]{1,0:T(4,128)}, s32[4,32]{1,0:T(4,128)S(1)}, u32[]{:S(2)}, u32[]{:S(2)}) collective-permute-start(s32[4,32]{1,0:T(4,128)} %refs_0_.1), channel_id=1, source_target_pairs={{0,2},{1,511},{2,4},{3,1},{4,6},{5,3},{6,8},{7,5},{8,10},{9,7},{10... | collective-permute-start | bytes 1544 | tf_op jit(solution)/shard_map/ppermute | solution.py:190
  16.9 1.9 %collective-permute-start.1 = (s32[4,32]{1,0:T(4,128)}, s32[4,32]{1,0:T(4,128)S(1)}, u32[]{:S(2)}, u32[]{:S(2)}) collective-permute-start(s32[4,32]{1,0:T(4,128)} %refs_0_.1), channel_id=1, source_target_pairs={{1,2},{0,511},{3,4},{2,1},{5,6},{4,3},{7,8},{6,5},{9,10},{8,7},{11... | collective-permute-start | bytes 1544 | tf_op jit(solution)/shard_map/ppermute | solution.py:191
  18.8 0.0 copy-done.7
  18.9 0.0 copy-done.8
  18.9 0.0 copy-done.6
  18.9 0.0 copy-done.5
  18.9 0.0 copy-done.4
  18.9 0.0 copy-done.3
  18.9 0.7 %pack.1.mine_ref = f32[4,16,256]{2,1,0:T(8,128)S(1)} custom-call(f32[8,128]{1,0:T(8,128)S(1)} %mark.1.mark_ref, s32[4]{0:T(128)S(1)} %bitcast.1, s32[4,32]{1,0:T(4,128)S(1)} %copy-done.7, s32[4,4,256]{2,1,0:T(4,128)S(1)} %copy-done.3, bf16[4,4,256]{2,1,0:T(4,128)(2,1)S(1)} %copy-done.4, s32[4,256]{1,0:T(4,128)S(1)} %copy-done.5, f32[4,256]{1,0:T(4,128)S(1)} %copy-done.6), custom_call_target="tpu_custom_call" | custom-call | flops 16384 | bytes 32768 | tf_op jit(solution)/shard_map/pack/pallas_call | solution.py:193
  19.6 0.0 copy-start.1
  19.6 0.0 copy-start.2
  19.6 0.0 collective-permute-done.first_ref
  19.6 2.4 %collective-permute-done.1.second_ref = s32[4,32]{1,0:T(4,128)S(1)} collective-permute-done((s32[4,32]{1,0:T(4,128)}, s32[4,32]{1,0:T(4,128)S(1)}, u32[]{:S(2)}, u32[]{:S(2)}) %collective-permute-start.1) | collective-permute-done | bytes 544 | tf_op jit(solution)/shard_map/ppermute | solution.py:191
  22.0 0.0 copy-done
  22.0 1.3 %serve.1 = bf16[256,384]{1,0:T(8,128)(2,1)S(1)} custom-call(s32[4,32]{1,0:T(4,128)S(1)} %collective-permute-done.first_ref, s32[4,32]{1,0:T(4,128)S(1)} %collective-permute-done.1.second_ref, bf16[4096,384]{1,0:T(8,128)(2,1)S(1)} %copy-done), custom_call_target="tpu_custom_call" | custom-call | flops 805306368 | bytes 3145728 | tf_op jit(solution)/shard_map/serve/pallas_call | solution.py:204
  23.3 2.0 %collective-permute-start.3 = (bf16[256,384]{1,0:T(8,128)(2,1)S(1)}, bf16[256,384]{1,0:T(8,128)(2,1)S(1)}, u32[]{:S(2)}, u32[]{:S(2)}) collective-permute-start(bf16[256,384]{1,0:T(8,128)(2,1)S(1)} %serve.1), channel_id=1, source_target_pairs={{2,1},{511,0},{4,3},{1,2},{6,5},{3,4},{8,7},{5,6},{10,9},{7,8},{12... | collective-permute-start | bytes 589832 | tf_op jit(solution)/shard_map/ppermute | solution.py:216
  25.3 1.9 %collective-permute-start.2 = (bf16[256,384]{1,0:T(8,128)(2,1)S(1)}, bf16[256,384]{1,0:T(8,128)(2,1)S(1)}, u32[]{:S(2)}, u32[]{:S(2)}) collective-permute-start(bf16[256,384]{1,0:T(8,128)(2,1)S(1)} %serve.1), channel_id=1, source_target_pairs={{2,0},{511,1},{4,2},{1,3},{6,4},{3,5},{8,6},{5,7},{10,8},{7,9},{12... | collective-permute-start | bytes 589832 | tf_op jit(solution)/shard_map/ppermute | solution.py:215
  27.2 8.2 %collective-permute-start.4 = (f32[4,16,256]{2,1,0:T(8,128)S(1)}, f32[4,16,256]{2,1,0:T(8,128)S(1)}, u32[]{:S(2)}, u32[]{:S(2)}) collective-permute-start(f32[4,16,256]{2,1,0:T(8,128)S(1)} %pack.1.mine_ref), channel_id=1, source_target_pairs={{0,1},{1,0},{2,3},{3,2},{4,5},{5,4},{6,7},{7,6},{8,9},{9,8},{10,11... | collective-permute-start | bytes 196616 | tf_op jit(solution)/shard_map/ppermute | solution.py:217
  35.5 0.9 %collective-permute-done.4.theirs_ref = f32[4,16,256]{2,1,0:T(8,128)S(1)} collective-permute-done((f32[4,16,256]{2,1,0:T(8,128)S(1)}, f32[4,16,256]{2,1,0:T(8,128)S(1)}, u32[]{:S(2)}, u32[]{:S(2)}) %collective-permute-start.4) | collective-permute-done | bytes 65568 | tf_op jit(solution)/shard_map/ppermute | solution.py:217
  36.4 1.2 %plan.1 = (bf16[192,384]{1,0:T(8,128)(2,1)S(1)}, bf16[192,256]{1,0:T(8,128)(2,1)S(1)}, bf16[192,256]{1,0:T(8,128)(2,1)S(1)}, bf16[6,256,64]{2,1,0:T(8,128)(2,1)S(1)}) custom-call(f32[4,16,256]{2,1,0:T(8,128)S(1)} %pack.1.mine_ref, f32[4,16,256]{2,1,0:T(8,128)S(1)} %collective-permute-done.4.theirs_ref, bf16[4096,384]{1,0:T(8,128)(2,1)S(1)} %copy-done), custom_call_target="tpu_custom_call" | custom-call | flops 603979776 | bytes 3145728 | tf_op jit(solution)/shard_map/plan/pallas_call | solution.py:219
  37.5 0.0 collective-permute-done.3.far_ref
  37.6 0.0 collective-permute-done.2.near_ref
  37.6 0.0 copy-done.1
  37.6 0.0 copy-done.2
  37.6 2.3 %ribbon.1 = bf16[1536,768]{1,0:T(8,128)(2,1)} custom-call(bf16[256,384]{1,0:T(8,128)(2,1)S(1)} %collective-permute-done.2.near_ref, bf16[256,384]{1,0:T(8,128)(2,1)S(1)} %collective-permute-done.3.far_ref, bf16[192,384]{1,0:T(8,128)(2,1)S(1)} %get-tuple-element.17.own_ref, bf16[192,256]{1,0:T(8,128)(2,1)S(1)} %get-tuple-element.18.sel_r_ref, ...), custom_call_target="tpu_custom_call" | custom-call | flops 603979776 | bytes 2359296 | tf_op jit(solution)/shard_map/ribbon/pallas_call | solution.py:234
  (1 shorter events, 0.0 us)
Async XLA Ops:
  0.0 18.8 %copy-start.7 = (s32[4,32]{1,0:T(4,128)S(1)}, s32[4,32]{1,0:T(4,128)}, u32[]{:S(2)}) copy-start(s32[4,32]{1,0:T(4,128)} %refs_0_.1) | copy-start | bytes 1540
  0.0 18.9 %copy-start.8 = (s32[4,1]{0,1:T(1,128)S(1)}, s32[4,1]{0,1:T(1,128)}, u32[]{:S(2)}) copy-start(s32[4,1]{0,1:T(1,128)} %param.15) | copy-start | bytes 52
  0.0 18.9 %copy-start.6 = (f32[4,256]{1,0:T(4,128)S(1)}, f32[4,256]{1,0:T(4,128)}, u32[]{:S(2)}) copy-start(f32[4,256]{1,0:T(4,128)} %refs_4_.1) | copy-start | bytes 12292
  0.0 18.9 %copy-start.5 = (s32[4,256]{1,0:T(4,128)S(1)}, s32[4,256]{1,0:T(4,128)}, u32[]{:S(2)}) copy-start(s32[4,256]{1,0:T(4,128)} %refs_3_.1) | copy-start | bytes 12292
  0.0 18.9 %copy-start.4 = (bf16[4,4,256]{2,1,0:T(4,128)(2,1)S(1)}, bf16[4,4,256]{2,1,0:T(4,128)(2,1)}, u32[]{:S(2)}) copy-start(bf16[4,4,256]{2,1,0:T(4,128)(2,1)} %refs_2_.1) | copy-start | bytes 24580
  0.0 18.9 %copy-start.3 = (s32[4,4,256]{2,1,0:T(4,128)S(1)}, s32[4,4,256]{2,1,0:T(4,128)}, u32[]{:S(2)}) copy-start(s32[4,4,256]{2,1,0:T(4,128)} %refs_1_.1) | copy-start | bytes 49156
  0.0 22.0 %copy-start = (bf16[4096,384]{1,0:T(8,128)(2,1)S(1)}, bf16[4096,384]{1,0:T(8,128)(2,1)}, u32[]{:S(2)}) copy-start(bf16[4096,384]{1,0:T(8,128)(2,1)} %table_ref.3) | copy-start | bytes 9437188
  0.0 19.5 %collective-permute-start = (s32[4,32]{1,0:T(4,128)}, s32[4,32]{1,0:T(4,128)S(1)}, u32[]{:S(2)}, u32[]{:S(2)}) collective-permute-start(s32[4,32]{1,0:T(4,128)} %refs_0_.1), channel_id=1, source_target_pairs={{0,2},{1,511},{2,4},{3,1},{4,6},{5,3},{6,8},{7,5},{8,10},{9,7},{10... | collective-permute-start | bytes 1544 | tf_op jit(solution)/shard_map/ppermute | solution.py:190
  16.9 5.1 %collective-permute-start.1 = (s32[4,32]{1,0:T(4,128)}, s32[4,32]{1,0:T(4,128)S(1)}, u32[]{:S(2)}, u32[]{:S(2)}) collective-permute-start(s32[4,32]{1,0:T(4,128)} %refs_0_.1), channel_id=1, source_target_pairs={{1,2},{0,511},{3,4},{2,1},{5,6},{4,3},{7,8},{6,5},{9,10},{8,7},{11... | collective-permute-start | bytes 1544 | tf_op jit(solution)/shard_map/ppermute | solution.py:191
  19.6 18.0 %copy-start.1 = (bf16[1,384,768]{2,1,0:T(8,128)(2,1)S(1)}, bf16[1,384,768]{2,1,0:T(8,128)(2,1)}, u32[]{:S(2)}) copy-start(bf16[1,384,768]{2,1,0:T(8,128)(2,1)} %centre_ref.1) | copy-start | bytes 1769476
  19.6 18.0 %copy-start.2 = (bf16[1,384,768]{2,1,0:T(8,128)(2,1)S(1)}, bf16[1,384,768]{2,1,0:T(8,128)(2,1)}, u32[]{:S(2)}) copy-start(bf16[1,384,768]{2,1,0:T(8,128)(2,1)} %side_ref.1) | copy-start | bytes 1769476
  23.3 14.2 %collective-permute-start.3 = (bf16[256,384]{1,0:T(8,128)(2,1)S(1)}, bf16[256,384]{1,0:T(8,128)(2,1)S(1)}, u32[]{:S(2)}, u32[]{:S(2)}) collective-permute-start(bf16[256,384]{1,0:T(8,128)(2,1)S(1)} %serve.1), channel_id=1, source_target_pairs={{2,1},{511,0},{4,3},{1,2},{6,5},{3,4},{8,7},{5,6},{10,9},{7,8},{12... | collective-permute-start | bytes 589832 | tf_op jit(solution)/shard_map/ppermute | solution.py:216
  25.3 12.3 %collective-permute-start.2 = (bf16[256,384]{1,0:T(8,128)(2,1)S(1)}, bf16[256,384]{1,0:T(8,128)(2,1)S(1)}, u32[]{:S(2)}, u32[]{:S(2)}) collective-permute-start(bf16[256,384]{1,0:T(8,128)(2,1)S(1)} %serve.1), channel_id=1, source_target_pairs={{2,0},{511,1},{4,2},{1,3},{6,4},{3,5},{8,6},{5,7},{10,8},{7,9},{12... | collective-permute-start | bytes 589832 | tf_op jit(solution)/shard_map/ppermute | solution.py:215
  27.2 9.1 %collective-permute-start.4 = (f32[4,16,256]{2,1,0:T(8,128)S(1)}, f32[4,16,256]{2,1,0:T(8,128)S(1)}, u32[]{:S(2)}, u32[]{:S(2)}) collective-permute-start(f32[4,16,256]{2,1,0:T(8,128)S(1)} %pack.1.mine_ref), channel_id=1, source_target_pairs={{0,1},{1,0},{2,3},{3,2},{4,5},{5,4},{6,7},{7,6},{8,9},{9,8},{10,11... | collective-permute-start | bytes 196616 | tf_op jit(solution)/shard_map/ppermute | solution.py:217
where the time goes:
time: 40.1 us; the launch traced here: 39.8 us
  starting transfers between devices  30.9 us (77%)
  Pallas kernels  5.41 us (13%)
  waiting for transfers between devices  3.3 us (8%)
    ppermute x1, starting transfers between devices, body(): first = lax.ppermute(neighbours, both, ask_pairs)  16.8 us
    ppermute x1, starting transfers between devices, body(): theirs = lax.ppermute(packed, 'screen', swap)  8.24 us
    ppermute x1, waiting for transfers between devices, body(): second = lax.ppermute(neighbours, both, cross_pairs)  2.42 us
    pallas_call x1, Pallas kernels, body(): pl.pallas_call(ribbon_kernel, out_shape=jax.ShapeDtypeStruct((total * str...  2.26 us
    ppermute x1, starting transfers between devices, body(): far = lax.ppermute(served, both, pass_pairs)  1.95 us
    ppermute x1, starting transfers between devices, body(): near = lax.ppermute(served, both, reply_pairs)  1.92 us
    ppermute x1, starting transfers between devices, body(): second = lax.ppermute(neighbours, both, cross_pairs)  1.92 us
    pallas_call x1, Pallas kernels, body(): pl.pallas_call(serve_kernel, out_shape=jax.ShapeDtypeStruct((all_rows, de...  1.31 us
  transfers between devices with their start and end apart: 5, of which 2 were waited for; matrix products, arithmetic and copies ran while one was open for 0% of the time, Pallas kernels for 5%

commit v1 on v0

--- a/solution.py
+++ b/solution.py
@@ -32,19 +32,22 @@
         hot_ref[:, part * CHUNK : (part + 1) * CHUNK] = jnp.where(key == lanes, 1.0, 0.0).astype(BF16)
 
 
-def serve_kernel(first_ref, second_ref, table_ref, out_ref, hot_ref):
-    listed = first_ref.shape[1]
+def serve_kernel(ask_ref, table_ref, *refs):
+    *before, out_ref, hot_ref = refs
+    blocks, listed = ask_ref.shape
     tile = table_ref.shape[0]
-    ask = jnp.concatenate([first_ref[...], second_ref[...]], axis=0)
-    blocks = ask.shape[0]
-    within = jnp.bitwise_and(ask, tile - 1).astype(F32)
+    within = jnp.bitwise_and(ask_ref[...], tile - 1).astype(F32)
     wide = jnp.concatenate(
         [jnp.broadcast_to(within[b : b + 1, :], (listed, listed)) for b in range(blocks)], axis=0
     )
     on = jnp.bitwise_and(iota(wide.shape, 0), listed - 1) == iota(wide.shape, 1)
     index = jnp.sum(jnp.where(on, wide, 0.0), axis=1, keepdims=True)
     fill_hot(hot_ref, index, None)
-    out_ref[...] = jnp.dot(hot_ref[...], table_ref[...], preferred_element_type=F32).astype(BF16)
+    rows = jnp.dot(hot_ref[...], table_ref[...], preferred_element_type=F32).astype(BF16)
+    start = out_ref.shape[0] - rows.shape[0]
+    for ref in before:
+        out_ref[:start, :] = ref[...]
+    out_ref[start:, :] = rows
 
 
 def mark_kernel(out_ref):
@@ -201,16 +204,21 @@
     )(mark, route[:, 0], *parts)
     first, packed = lax.optimization_barrier((first, packed))
     all_rows = 2 * blocks * listed
-    served = pl.pallas_call(
-        serve_kernel,
-        out_shape=jax.ShapeDtypeStruct((all_rows, depth), BF16),
-        in_specs=[VMEM, VMEM, VMEM],
-        out_specs=VMEM,
-        scratch_shapes=[pltpu.VMEM((all_rows, tile), BF16)],
-        cost_estimate=cost(2 * all_rows * tile * depth, tile * depth * 2),
-        compiler_params=pltpu.CompilerParams(vmem_limit_bytes=LIMIT),
-        name="serve",
-    )(first, second, guides)
+    half_rows = all_rows // 2
+
+    def serve(rows, *operands):
+        return pl.pallas_call(
+            serve_kernel,
+            out_shape=jax.ShapeDtypeStruct((rows, depth), BF16),
+            in_specs=[VMEM] * len(operands),
+            out_specs=VMEM,
+            scratch_shapes=[pltpu.VMEM((half_rows, tile), BF16)],
+            cost_estimate=cost(2 * half_rows * tile * depth, tile * depth * 2),
+            compiler_params=pltpu.CompilerParams(vmem_limit_bytes=LIMIT),
+        )(*operands)
+
+    served = serve(half_rows, first, guides)
+    served = serve(all_rows, second, guides, served)
     served, packed = lax.optimization_barrier((served, packed))
     near = lax.ppermute(served, both, reply_pairs)
     far = lax.ppermute(served, both, pass_pairs)

time: 40.1 us -> 46.3 us (1.15)
  waiting for transfers between devices: 3.3 us -> 7.06 us
  starting transfers between devices: 30.9 us -> 33.2 us
    ppermute x1, waiting for transfers between devices: 0.01 us -> 5.99 us  [body(): near = lax.ppermute(served, both, reply_pairs)]
    ppermute x1, starting transfers between devices: 1.92 us -> 4.76 us  [body(): second = lax.ppermute(neighbours, both, cross_pairs)]
    ppermute x1, starting transfers between devices: 16.8 us -> 14 us  [body(): first = lax.ppermute(neighbours, both, ask_pairs)]
    ppermute x1, starting transfers between devices: 1.95 us -> 4.76 us  [body(): far = lax.ppermute(served, both, pass_pairs)]
    ppermute x1, waiting for transfers between devices: 2.42 us -> 0.01 us  [body(): second = lax.ppermute(neighbours, both, cross_pairs)]
    ppermute x1, starting transfers between devices: 8.24 us -> 7.73 us  [body(): theirs = lax.ppermute(packed, 'screen', swap)]
    pallas_call x1 -> x2, Pallas kernels: 1.31 us -> 1.54 us  [serve(): pl.pallas_call(serve_kernel, out_shape=jax.ShapeDtypeStruct((rows, depth)...]
  transfers between devices with their start and end apart: 5 -> 5, of which waited for: 2 -> 3; matrix products, arithmetic and copies ran while one was open for 0% -> 0% of each run, Pallas kernels for 5% -> 6%
where the time goes in v1:
time: 46.3 us; the launch traced here: 46.1 us
  starting transfers between devices  33.2 us (72%)
  waiting for transfers between devices  7.06 us (15%)
  Pallas kernels  5.64 us (12%)
    ppermute x1, starting transfers between devices, body(): first = lax.ppermute(neighbours, both, ask_pairs)  14 us
    ppermute x1, starting transfers between devices, body(): theirs = lax.ppermute(packed, 'screen', swap)  7.73 us
    ppermute x1, waiting for transfers between devices, body(): near = lax.ppermute(served, both, reply_pairs)  5.99 us
    ppermute x1, starting transfers between devices, body(): second = lax.ppermute(neighbours, both, cross_pairs)  4.76 us
    ppermute x1, starting transfers between devices, body(): far = lax.ppermute(served, both, pass_pairs)  4.76 us
    pallas_call x1, Pallas kernels, body(): pl.pallas_call(ribbon_kernel, out_shape=jax.ShapeDtypeStruct((total * str...  2.26 us
    ppermute x1, starting transfers between devices, body(): near = lax.ppermute(served, both, reply_pairs)  1.92 us
    pallas_call x2, Pallas kernels, serve(): pl.pallas_call(serve_kernel, out_shape=jax.ShapeDtypeStruct((rows, depth)...  1.54 us
  transfers between devices with their start and end apart: 5, of which 3 were waited for; matrix products, arithmetic and copies ran while one was open for 0% of the time, Pallas kernels for 6%

profile of v1, /device:TPU:1, one launch (start us, length us, event | category | flops | bytes accessed | tf_op | source)
XLA Modules:
  0.0 46.1 jit_solution(3538289133683564208)
XLA Ops:
  0.0 0.0 copy-start.7
  0.0 0.0 copy-start.8
  0.0 0.0 copy-start.6
  0.0 0.0 copy-start.5
  0.0 0.0 copy-start.4
  0.0 0.0 copy-start.3
  0.0 0.0 copy-start
  0.0 4.8 %collective-permute-start = (s32[4,32]{1,0:T(4,128)}, s32[4,32]{1,0:T(4,128)S(1)}, u32[]{:S(2)}, u32[]{:S(2)}) collective-permute-start(s32[4,32]{1,0:T(4,128)} %refs_0_.1), channel_id=1, source_target_pairs={{1,2},{0,511},{3,4},{2,1},{5,6},{4,3},{7,8},{6,5},{9,10},{8,7},{11... | collective-permute-start | bytes 1544 | tf_op jit(solution)/shard_map/ppermute | solution.py:194
  4.8 14.0 %collective-permute-start.1 = (s32[4,32]{1,0:T(4,128)}, s32[4,32]{1,0:T(4,128)S(1)}, u32[]{:S(2)}, u32[]{:S(2)}) collective-permute-start(s32[4,32]{1,0:T(4,128)} %refs_0_.1), channel_id=1, source_target_pairs={{0,2},{1,511},{2,4},{3,1},{4,6},{5,3},{6,8},{7,5},{8,10},{9,7},{10... | collective-permute-start | bytes 1544 | tf_op jit(solution)/shard_map/ppermute | solution.py:193
  18.8 0.0 copy-done.7
  18.9 0.0 copy-done.8
  18.9 0.0 copy-done.6
  18.9 0.0 copy-done.5
  18.9 0.0 copy-done.4
  18.9 0.0 copy-done.3
  18.9 0.7 %pack.1.mine_ref = f32[4,16,256]{2,1,0:T(8,128)S(1)} custom-call(f32[8,128]{1,0:T(8,128)S(1)} %mark.1.mark_ref, s32[4]{0:T(128)S(1)} %bitcast.1, s32[4,32]{1,0:T(4,128)S(1)} %copy-done.7, s32[4,4,256]{2,1,0:T(4,128)S(1)} %copy-done.3, bf16[4,4,256]{2,1,0:T(4,128)(2,1)S(1)} %copy-done.4, s32[4,256]{1,0:T(4,128)S(1)} %copy-done.5, f32[4,256]{1,0:T(4,128)S(1)} %copy-done.6), custom_call_target="tpu_custom_call" | custom-call | flops 16384 | bytes 32768 | tf_op jit(solution)/shard_map/pack/pallas_call | solution.py:196
  19.6 0.2 collective-permute-done.1.ask_ref
  19.8 0.0 copy-done
  19.8 0.8 %shard_map.91.refs_0_ = bf16[128,384]{1,0:T(8,128)(2,1)S(1)} custom-call(s32[4,32]{1,0:T(4,128)S(1)} %collective-permute-done.1.ask_ref, bf16[4096,384]{1,0:T(8,128)(2,1)S(1)} %copy-done), custom_call_target="tpu_custom_call" | custom-call | flops 402653184 | bytes 3145728 | tf_op jit(solution)/shard_map/pallas_call | solution.py:210
  20.5 0.0 copy-start.1
  20.6 0.0 copy-start.2
  20.6 0.0 collective-permute-done.ask_ref
  20.6 0.8 %shard_map.92 = bf16[256,384]{1,0:T(8,128)(2,1)S(1)} custom-call(s32[4,32]{1,0:T(4,128)S(1)} %collective-permute-done.ask_ref, bf16[4096,384]{1,0:T(8,128)(2,1)S(1)} %copy-done, bf16[128,384]{1,0:T(8,128)(2,1)S(1)} %shard_map.91.refs_0_), custom_call_target="tpu_custom_call" | custom-call | flops 402653184 | bytes 3145728 | tf_op jit(solution)/shard_map/pallas_call | solution.py:210
  21.4 4.8 %collective-permute-start.3 = (bf16[256,384]{1,0:T(8,128)(2,1)S(1)}, bf16[256,384]{1,0:T(8,128)(2,1)S(1)}, u32[]{:S(2)}, u32[]{:S(2)}) collective-permute-start(bf16[256,384]{1,0:T(8,128)(2,1)S(1)} %shard_map.92), channel_id=1, source_target_pairs={{2,1},{511,0},{4,3},{1,2},{6,5},{3,4},{8,7},{5,6},{10,9},{7,8},{12... | collective-permute-start | bytes 589832 | tf_op jit(solution)/shard_map/ppermute | solution.py:224
  26.1 1.9 %collective-permute-start.2 = (bf16[256,384]{1,0:T(8,128)(2,1)S(1)}, bf16[256,384]{1,0:T(8,128)(2,1)S(1)}, u32[]{:S(2)}, u32[]{:S(2)}) collective-permute-start(bf16[256,384]{1,0:T(8,128)(2,1)S(1)} %shard_map.92), channel_id=1, source_target_pairs={{2,0},{511,1},{4,2},{1,3},{6,4},{3,5},{8,6},{5,7},{10,8},{7,9},{12... | collective-permute-start | bytes 589832 | tf_op jit(solution)/shard_map/ppermute | solution.py:223
  28.1 7.7 %collective-permute-start.4 = (f32[4,16,256]{2,1,0:T(8,128)S(1)}, f32[4,16,256]{2,1,0:T(8,128)S(1)}, u32[]{:S(2)}, u32[]{:S(2)}) collective-permute-start(f32[4,16,256]{2,1,0:T(8,128)S(1)} %pack.1.mine_ref), channel_id=1, source_target_pairs={{0,1},{1,0},{2,3},{3,2},{4,5},{5,4},{6,7},{7,6},{8,9},{9,8},{10,11... | collective-permute-start | bytes 196616 | tf_op jit(solution)/shard_map/ppermute | solution.py:225
  35.8 0.9 %collective-permute-done.4.theirs_ref = f32[4,16,256]{2,1,0:T(8,128)S(1)} collective-permute-done((f32[4,16,256]{2,1,0:T(8,128)S(1)}, f32[4,16,256]{2,1,0:T(8,128)S(1)}, u32[]{:S(2)}, u32[]{:S(2)}) %collective-permute-start.4) | collective-permute-done | bytes 65568 | tf_op jit(solution)/shard_map/ppermute | solution.py:225
  36.7 1.2 %plan.1 = (bf16[192,384]{1,0:T(8,128)(2,1)S(1)}, bf16[192,256]{1,0:T(8,128)(2,1)S(1)}, bf16[192,256]{1,0:T(8,128)(2,1)S(1)}, bf16[6,256,64]{2,1,0:T(8,128)(2,1)S(1)}) custom-call(f32[4,16,256]{2,1,0:T(8,128)S(1)} %pack.1.mine_ref, f32[4,16,256]{2,1,0:T(8,128)S(1)} %collective-permute-done.4.theirs_ref, bf16[4096,384]{1,0:T(8,128)(2,1)S(1)} %copy-done), custom_call_target="tpu_custom_call" | custom-call | flops 603979776 | bytes 3145728 | tf_op jit(solution)/shard_map/plan/pallas_call | solution.py:227
  37.9 0.0 collective-permute-done.3.far_ref
  37.9 6.0 %collective-permute-done.2.near_ref = bf16[256,384]{1,0:T(8,128)(2,1)S(1)} collective-permute-done((bf16[256,384]{1,0:T(8,128)(2,1)S(1)}, bf16[256,384]{1,0:T(8,128)(2,1)S(1)}, u32[]{:S(2)}, u32[]{:S(2)}) %collective-permute-start.2) | collective-permute-done | bytes 196640 | tf_op jit(solution)/shard_map/ppermute | solution.py:223
  43.9 0.0 copy-done.1
  43.9 0.0 copy-done.2
  43.9 2.3 %ribbon.1 = bf16[1536,768]{1,0:T(8,128)(2,1)} custom-call(bf16[256,384]{1,0:T(8,128)(2,1)S(1)} %collective-permute-done.2.near_ref, bf16[256,384]{1,0:T(8,128)(2,1)S(1)} %collective-permute-done.3.far_ref, bf16[192,384]{1,0:T(8,128)(2,1)S(1)} %get-tuple-element.17.own_ref, bf16[192,256]{1,0:T(8,128)(2,1)S(1)} %get-tuple-element.18.sel_r_ref, ...), custom_call_target="tpu_custom_call" | custom-call | flops 603979776 | bytes 2359296 | tf_op jit(solution)/shard_map/ribbon/pallas_call | solution.py:242
  (1 shorter events, 0.0 us)
Async XLA Ops:
  0.0 18.8 %copy-start.7 = (s32[4,32]{1,0:T(4,128)S(1)}, s32[4,32]{1,0:T(4,128)}, u32[]{:S(2)}) copy-start(s32[4,32]{1,0:T(4,128)} %refs_0_.1) | copy-start | bytes 1540
  0.0 18.9 %copy-start.8 = (s32[4,1]{0,1:T(1,128)S(1)}, s32[4,1]{0,1:T(1,128)}, u32[]{:S(2)}) copy-start(s32[4,1]{0,1:T(1,128)} %param.15) | copy-start | bytes 52
  0.0 18.9 %copy-start.6 = (f32[4,256]{1,0:T(4,128)S(1)}, f32[4,256]{1,0:T(4,128)}, u32[]{:S(2)}) copy-start(f32[4,256]{1,0:T(4,128)} %refs_4_.1) | copy-start | bytes 12292
  0.0 18.9 %copy-start.5 = (s32[4,256]{1,0:T(4,128)S(1)}, s32[4,256]{1,0:T(4,128)}, u32[]{:S(2)}) copy-start(s32[4,256]{1,0:T(4,128)} %refs_3_.1) | copy-start | bytes 12292
  0.0 18.9 %copy-start.4 = (bf16[4,4,256]{2,1,0:T(4,128)(2,1)S(1)}, bf16[4,4,256]{2,1,0:T(4,128)(2,1)}, u32[]{:S(2)}) copy-start(bf16[4,4,256]{2,1,0:T(4,128)(2,1)} %refs_2_.1) | copy-start | bytes 24580
  0.0 18.9 %copy-start.3 = (s32[4,4,256]{2,1,0:T(4,128)S(1)}, s32[4,4,256]{2,1,0:T(4,128)}, u32[]{:S(2)}) copy-start(s32[4,4,256]{2,1,0:T(4,128)} %refs_1_.1) | copy-start | bytes 49156
  0.0 19.7 %copy-start = (bf16[4096,384]{1,0:T(8,128)(2,1)S(1)}, bf16[4096,384]{1,0:T(8,128)(2,1)}, u32[]{:S(2)}) copy-start(bf16[4096,384]{1,0:T(8,128)(2,1)} %table_ref.5) | copy-start | bytes 9437188
  0.0 20.5 %collective-permute-start = (s32[4,32]{1,0:T(4,128)}, s32[4,32]{1,0:T(4,128)S(1)}, u32[]{:S(2)}, u32[]{:S(2)}) collective-permute-start(s32[4,32]{1,0:T(4,128)} %refs_0_.1), channel_id=1, source_target_pairs={{1,2},{0,511},{3,4},{2,1},{5,6},{4,3},{7,8},{6,5},{9,10},{8,7},{11... | collective-permute-start | bytes 1544 | tf_op jit(solution)/shard_map/ppermute | solution.py:194
  4.8 14.9 %collective-permute-start.1 = (s32[4,32]{1,0:T(4,128)}, s32[4,32]{1,0:T(4,128)S(1)}, u32[]{:S(2)}, u32[]{:S(2)}) collective-permute-start(s32[4,32]{1,0:T(4,128)} %refs_0_.1), channel_id=1, source_target_pairs={{0,2},{1,511},{2,4},{3,1},{4,6},{5,3},{6,8},{7,5},{8,10},{9,7},{10... | collective-permute-start | bytes 1544 | tf_op jit(solution)/shard_map/ppermute | solution.py:193
  20.5 23.3 %copy-start.1 = (bf16[1,384,768]{2,1,0:T(8,128)(2,1)S(1)}, bf16[1,384,768]{2,1,0:T(8,128)(2,1)}, u32[]{:S(2)}) copy-start(bf16[1,384,768]{2,1,0:T(8,128)(2,1)} %centre_ref.1) | copy-start | bytes 1769476
  20.6 23.3 %copy-start.2 = (bf16[1,384,768]{2,1,0:T(8,128)(2,1)S(1)}, bf16[1,384,768]{2,1,0:T(8,128)(2,1)}, u32[]{:S(2)}) copy-start(bf16[1,384,768]{2,1,0:T(8,128)(2,1)} %side_ref.1) | copy-start | bytes 1769476
  21.4 16.5 %collective-permute-start.3 = (bf16[256,384]{1,0:T(8,128)(2,1)S(1)}, bf16[256,384]{1,0:T(8,128)(2,1)S(1)}, u32[]{:S(2)}, u32[]{:S(2)}) collective-permute-start(bf16[256,384]{1,0:T(8,128)(2,1)S(1)} %shard_map.92), channel_id=1, source_target_pairs={{2,1},{511,0},{4,3},{1,2},{6,5},{3,4},{8,7},{5,6},{10,9},{7,8},{12... | collective-permute-start | bytes 589832 | tf_op jit(solution)/shard_map/ppermute | solution.py:224
  26.1 17.7 %collective-permute-start.2 = (bf16[256,384]{1,0:T(8,128)(2,1)S(1)}, bf16[256,384]{1,0:T(8,128)(2,1)S(1)}, u32[]{:S(2)}, u32[]{:S(2)}) collective-permute-start(bf16[256,384]{1,0:T(8,128)(2,1)S(1)} %shard_map.92), channel_id=1, source_target_pairs={{2,0},{511,1},{4,2},{1,3},{6,4},{3,5},{8,6},{5,7},{10,8},{7,9},{12... | collective-permute-start | bytes 589832 | tf_op jit(solution)/shard_map/ppermute | solution.py:223
  28.1 8.6 %collective-permute-start.4 = (f32[4,16,256]{2,1,0:T(8,128)S(1)}, f32[4,16,256]{2,1,0:T(8,128)S(1)}, u32[]{:S(2)}, u32[]{:S(2)}) collective-permute-start(f32[4,16,256]{2,1,0:T(8,128)S(1)} %pack.1.mine_ref), channel_id=1, source_target_pairs={{0,1},{1,0},{2,3},{3,2},{4,5},{5,4},{6,7},{7,6},{8,9},{9,8},{10,11... | collective-permute-start | bytes 196616 | tf_op jit(solution)/shard_map/ppermute | solution.py:225

commit v2 on v1

--- a/solution.py
+++ b/solution.py
@@ -26,10 +26,11 @@
     high = jnp.floor(index * (1.0 / CHUNK))
     low = index - high * CHUNK
     low = low if valid is None else jnp.where(valid, low, -1.0)
-    lanes = iota((rows, CHUNK), 1).astype(F32)
+    lanes = iota((rows, CHUNK), 1).astype(F32).astype(BF16)
+    one, zero = jnp.array(1.0, BF16), jnp.array(0.0, BF16)
     for part in range(hot_ref.shape[1] // CHUNK):
-        key = jnp.where(high == part, low, -1.0)
-        hot_ref[:, part * CHUNK : (part + 1) * CHUNK] = jnp.where(key == lanes, 1.0, 0.0).astype(BF16)
+        key = jnp.where(high == part, low, -1.0).astype(BF16)
+        hot_ref[:, part * CHUNK : (part + 1) * CHUNK] = jnp.where(key == lanes, one, zero)
 
 
 def serve_kernel(ask_ref, table_ref, *refs):

time: 46.3 us -> 46.3 us (level)
  no operation moved by 1% of the time
where the time goes in v2:
time: 46.3 us; the launch traced here: 46.1 us
  starting transfers between devices  33.2 us (72%)
  waiting for transfers between devices  7.07 us (15%)
  Pallas kernels  5.63 us (12%)
    ppermute x1, starting transfers between devices, body(): first = lax.ppermute(neighbours, both, ask_pairs)  14 us
    ppermute x1, starting transfers between devices, body(): theirs = lax.ppermute(packed, 'screen', swap)  7.73 us
    ppermute x1, waiting for transfers between devices, body(): near = lax.ppermute(served, both, reply_pairs)  6 us
    ppermute x1, starting transfers between devices, body(): far = lax.ppermute(served, both, pass_pairs)  4.76 us
    ppermute x1, starting transfers between devices, body(): second = lax.ppermute(neighbours, both, cross_pairs)  4.76 us
    pallas_call x1, Pallas kernels, body(): pl.pallas_call(ribbon_kernel, out_shape=jax.ShapeDtypeStruct((total * str...  2.26 us
    ppermute x1, starting transfers between devices, body(): near = lax.ppermute(served, both, reply_pairs)  1.92 us
    pallas_call x2, Pallas kernels, serve(): pl.pallas_call(serve_kernel, out_shape=jax.ShapeDtypeStruct((rows, depth)...  1.54 us
  transfers between devices with their start and end apart: 5, of which 3 were waited for; matrix products, arithmetic and copies ran while one was open for 0% of the time, Pallas kernels for 6%

profile of v2, /device:TPU:1, one launch (start us, length us, event | category | flops | bytes accessed | tf_op | source)
XLA Modules:
  0.0 46.1 jit_solution(15537935190029523103)
XLA Ops:
  0.0 0.0 copy-start.7
  0.0 0.0 copy-start.8
  0.0 0.0 copy-start.6
  0.0 0.0 copy-start.5
  0.0 0.0 copy-start.4
  0.0 0.0 copy-start.3
  0.0 0.0 copy-start
  0.0 4.8 %collective-permute-start = (s32[4,32]{1,0:T(4,128)}, s32[4,32]{1,0:T(4,128)S(1)}, u32[]{:S(2)}, u32[]{:S(2)}) collective-permute-start(s32[4,32]{1,0:T(4,128)} %refs_0_.1), channel_id=1, source_target_pairs={{1,2},{0,511},{3,4},{2,1},{5,6},{4,3},{7,8},{6,5},{9,10},{8,7},{11... | collective-permute-start | bytes 1544 | tf_op jit(solution)/shard_map/ppermute | solution.py:195
  4.8 14.0 %collective-permute-start.1 = (s32[4,32]{1,0:T(4,128)}, s32[4,32]{1,0:T(4,128)S(1)}, u32[]{:S(2)}, u32[]{:S(2)}) collective-permute-start(s32[4,32]{1,0:T(4,128)} %refs_0_.1), channel_id=1, source_target_pairs={{0,2},{1,511},{2,4},{3,1},{4,6},{5,3},{6,8},{7,5},{8,10},{9,7},{10... | collective-permute-start | bytes 1544 | tf_op jit(solution)/shard_map/ppermute | solution.py:194
  18.8 0.0 copy-done.7
  18.9 0.0 copy-done.8
  18.9 0.0 copy-done.6
  18.9 0.0 copy-done.5
  18.9 0.0 copy-done.4
  18.9 0.0 copy-done.3
  18.9 0.7 %pack.1.mine_ref = f32[4,16,256]{2,1,0:T(8,128)S(1)} custom-call(f32[8,128]{1,0:T(8,128)S(1)} %mark.1.mark_ref, s32[4]{0:T(128)S(1)} %bitcast.1, s32[4,32]{1,0:T(4,128)S(1)} %copy-done.7, s32[4,4,256]{2,1,0:T(4,128)S(1)} %copy-done.3, bf16[4,4,256]{2,1,0:T(4,128)(2,1)S(1)} %copy-done.4, s32[4,256]{1,0:T(4,128)S(1)} %copy-done.5, f32[4,256]{1,0:T(4,128)S(1)} %copy-done.6), custom_call_target="tpu_custom_call" | custom-call | flops 16384 | bytes 32768 | tf_op jit(solution)/shard_map/pack/pallas_call | solution.py:197
  19.6 0.2 collective-permute-done.1.ask_ref
  19.8 0.0 copy-done
  19.8 0.8 %shard_map.91.refs_0_ = bf16[128,384]{1,0:T(8,128)(2,1)S(1)} custom-call(s32[4,32]{1,0:T(4,128)S(1)} %collective-permute-done.1.ask_ref, bf16[4096,384]{1,0:T(8,128)(2,1)S(1)} %copy-done), custom_call_target="tpu_custom_call" | custom-call | flops 402653184 | bytes 3145728 | tf_op jit(solution)/shard_map/pallas_call | solution.py:211
  20.5 0.0 copy-start.1
  20.6 0.0 copy-start.2
  20.6 0.0 collective-permute-done.ask_ref
  20.6 0.8 %shard_map.92 = bf16[256,384]{1,0:T(8,128)(2,1)S(1)} custom-call(s32[4,32]{1,0:T(4,128)S(1)} %collective-permute-done.ask_ref, bf16[4096,384]{1,0:T(8,128)(2,1)S(1)} %copy-done, bf16[128,384]{1,0:T(8,128)(2,1)S(1)} %shard_map.91.refs_0_), custom_call_target="tpu_custom_call" | custom-call | flops 402653184 | bytes 3145728 | tf_op jit(solution)/shard_map/pallas_call | solution.py:211
  21.4 4.8 %collective-permute-start.3 = (bf16[256,384]{1,0:T(8,128)(2,1)S(1)}, bf16[256,384]{1,0:T(8,128)(2,1)S(1)}, u32[]{:S(2)}, u32[]{:S(2)}) collective-permute-start(bf16[256,384]{1,0:T(8,128)(2,1)S(1)} %shard_map.92), channel_id=1, source_target_pairs={{2,1},{511,0},{4,3},{1,2},{6,5},{3,4},{8,7},{5,6},{10,9},{7,8},{12... | collective-permute-start | bytes 589832 | tf_op jit(solution)/shard_map/ppermute | solution.py:225
  26.1 1.9 %collective-permute-start.2 = (bf16[256,384]{1,0:T(8,128)(2,1)S(1)}, bf16[256,384]{1,0:T(8,128)(2,1)S(1)}, u32[]{:S(2)}, u32[]{:S(2)}) collective-permute-start(bf16[256,384]{1,0:T(8,128)(2,1)S(1)} %shard_map.92), channel_id=1, source_target_pairs={{2,0},{511,1},{4,2},{1,3},{6,4},{3,5},{8,6},{5,7},{10,8},{7,9},{12... | collective-permute-start | bytes 589832 | tf_op jit(solution)/shard_map/ppermute | solution.py:224
  28.1 7.7 %collective-permute-start.4 = (f32[4,16,256]{2,1,0:T(8,128)S(1)}, f32[4,16,256]{2,1,0:T(8,128)S(1)}, u32[]{:S(2)}, u32[]{:S(2)}) collective-permute-start(f32[4,16,256]{2,1,0:T(8,128)S(1)} %pack.1.mine_ref), channel_id=1, source_target_pairs={{0,1},{1,0},{2,3},{3,2},{4,5},{5,4},{6,7},{7,6},{8,9},{9,8},{10,11... | collective-permute-start | bytes 196616 | tf_op jit(solution)/shard_map/ppermute | solution.py:226
  35.8 0.9 %collective-permute-done.4.theirs_ref = f32[4,16,256]{2,1,0:T(8,128)S(1)} collective-permute-done((f32[4,16,256]{2,1,0:T(8,128)S(1)}, f32[4,16,256]{2,1,0:T(8,128)S(1)}, u32[]{:S(2)}, u32[]{:S(2)}) %collective-permute-start.4) | collective-permute-done | bytes 65568 | tf_op jit(solution)/shard_map/ppermute | solution.py:226
  36.7 1.2 %plan.1 = (bf16[192,384]{1,0:T(8,128)(2,1)S(1)}, bf16[192,256]{1,0:T(8,128)(2,1)S(1)}, bf16[192,256]{1,0:T(8,128)(2,1)S(1)}, bf16[6,256,64]{2,1,0:T(8,128)(2,1)S(1)}) custom-call(f32[4,16,256]{2,1,0:T(8,128)S(1)} %pack.1.mine_ref, f32[4,16,256]{2,1,0:T(8,128)S(1)} %collective-permute-done.4.theirs_ref, bf16[4096,384]{1,0:T(8,128)(2,1)S(1)} %copy-done), custom_call_target="tpu_custom_call" | custom-call | flops 603979776 | bytes 3145728 | tf_op jit(solution)/shard_map/plan/pallas_call | solution.py:228
  37.8 0.0 collective-permute-done.3.far_ref
  37.9 6.0 %collective-permute-done.2.near_ref = bf16[256,384]{1,0:T(8,128)(2,1)S(1)} collective-permute-done((bf16[256,384]{1,0:T(8,128)(2,1)S(1)}, bf16[256,384]{1,0:T(8,128)(2,1)S(1)}, u32[]{:S(2)}, u32[]{:S(2)}) %collective-permute-start.2) | collective-permute-done | bytes 196640 | tf_op jit(solution)/shard_map/ppermute | solution.py:224
  43.9 0.0 copy-done.1
  43.9 0.0 copy-done.2
  43.9 2.3 %ribbon.1 = bf16[1536,768]{1,0:T(8,128)(2,1)} custom-call(bf16[256,384]{1,0:T(8,128)(2,1)S(1)} %collective-permute-done.2.near_ref, bf16[256,384]{1,0:T(8,128)(2,1)S(1)} %collective-permute-done.3.far_ref, bf16[192,384]{1,0:T(8,128)(2,1)S(1)} %get-tuple-element.17.own_ref, bf16[192,256]{1,0:T(8,128)(2,1)S(1)} %get-tuple-element.18.sel_r_ref, ...), custom_call_target="tpu_custom_call" | custom-call | flops 603979776 | bytes 2359296 | tf_op jit(solution)/shard_map/ribbon/pallas_call | solution.py:243
  (1 shorter events, 0.0 us)
Async XLA Ops:
  0.0 18.8 %copy-start.7 = (s32[4,32]{1,0:T(4,128)S(1)}, s32[4,32]{1,0:T(4,128)}, u32[]{:S(2)}) copy-start(s32[4,32]{1,0:T(4,128)} %refs_0_.1) | copy-start | bytes 1540
  0.0 18.9 %copy-start.8 = (s32[4,1]{0,1:T(1,128)S(1)}, s32[4,1]{0,1:T(1,128)}, u32[]{:S(2)}) copy-start(s32[4,1]{0,1:T(1,128)} %param.15) | copy-start | bytes 52
  0.0 18.9 %copy-start.6 = (f32[4,256]{1,0:T(4,128)S(1)}, f32[4,256]{1,0:T(4,128)}, u32[]{:S(2)}) copy-start(f32[4,256]{1,0:T(4,128)} %refs_4_.1) | copy-start | bytes 12292
  0.0 18.9 %copy-start.5 = (s32[4,256]{1,0:T(4,128)S(1)}, s32[4,256]{1,0:T(4,128)}, u32[]{:S(2)}) copy-start(s32[4,256]{1,0:T(4,128)} %refs_3_.1) | copy-start | bytes 12292
  0.0 18.9 %copy-start.4 = (bf16[4,4,256]{2,1,0:T(4,128)(2,1)S(1)}, bf16[4,4,256]{2,1,0:T(4,128)(2,1)}, u32[]{:S(2)}) copy-start(bf16[4,4,256]{2,1,0:T(4,128)(2,1)} %refs_2_.1) | copy-start | bytes 24580
  0.0 18.9 %copy-start.3 = (s32[4,4,256]{2,1,0:T(4,128)S(1)}, s32[4,4,256]{2,1,0:T(4,128)}, u32[]{:S(2)}) copy-start(s32[4,4,256]{2,1,0:T(4,128)} %refs_1_.1) | copy-start | bytes 49156
  0.0 19.7 %copy-start = (bf16[4096,384]{1,0:T(8,128)(2,1)S(1)}, bf16[4096,384]{1,0:T(8,128)(2,1)}, u32[]{:S(2)}) copy-start(bf16[4096,384]{1,0:T(8,128)(2,1)} %table_ref.5) | copy-start | bytes 9437188
  0.0 20.5 %collective-permute-start = (s32[4,32]{1,0:T(4,128)}, s32[4,32]{1,0:T(4,128)S(1)}, u32[]{:S(2)}, u32[]{:S(2)}) collective-permute-start(s32[4,32]{1,0:T(4,128)} %refs_0_.1), channel_id=1, source_target_pairs={{1,2},{0,511},{3,4},{2,1},{5,6},{4,3},{7,8},{6,5},{9,10},{8,7},{11... | collective-permute-start | bytes 1544 | tf_op jit(solution)/shard_map/ppermute | solution.py:195
  4.8 14.9 %collective-permute-start.1 = (s32[4,32]{1,0:T(4,128)}, s32[4,32]{1,0:T(4,128)S(1)}, u32[]{:S(2)}, u32[]{:S(2)}) collective-permute-start(s32[4,32]{1,0:T(4,128)} %refs_0_.1), channel_id=1, source_target_pairs={{0,2},{1,511},{2,4},{3,1},{4,6},{5,3},{6,8},{7,5},{8,10},{9,7},{10... | collective-permute-start | bytes 1544 | tf_op jit(solution)/shard_map/ppermute | solution.py:194
  20.5 23.3 %copy-start.1 = (bf16[1,384,768]{2,1,0:T(8,128)(2,1)S(1)}, bf16[1,384,768]{2,1,0:T(8,128)(2,1)}, u32[]{:S(2)}) copy-start(bf16[1,384,768]{2,1,0:T(8,128)(2,1)} %centre_ref.1) | copy-start | bytes 1769476
  20.6 23.3 %copy-start.2 = (bf16[1,384,768]{2,1,0:T(8,128)(2,1)S(1)}, bf16[1,384,768]{2,1,0:T(8,128)(2,1)}, u32[]{:S(2)}) copy-start(bf16[1,384,768]{2,1,0:T(8,128)(2,1)} %side_ref.1) | copy-start | bytes 1769476
  21.4 16.5 %collective-permute-start.3 = (bf16[256,384]{1,0:T(8,128)(2,1)S(1)}, bf16[256,384]{1,0:T(8,128)(2,1)S(1)}, u32[]{:S(2)}, u32[]{:S(2)}) collective-permute-start(bf16[256,384]{1,0:T(8,128)(2,1)S(1)} %shard_map.92), channel_id=1, source_target_pairs={{2,1},{511,0},{4,3},{1,2},{6,5},{3,4},{8,7},{5,6},{10,9},{7,8},{12... | collective-permute-start | bytes 589832 | tf_op jit(solution)/shard_map/ppermute | solution.py:225
  26.1 17.7 %collective-permute-start.2 = (bf16[256,384]{1,0:T(8,128)(2,1)S(1)}, bf16[256,384]{1,0:T(8,128)(2,1)S(1)}, u32[]{:S(2)}, u32[]{:S(2)}) collective-permute-start(bf16[256,384]{1,0:T(8,128)(2,1)S(1)} %shard_map.92), channel_id=1, source_target_pairs={{2,0},{511,1},{4,2},{1,3},{6,4},{3,5},{8,6},{5,7},{10,8},{7,9},{12... | collective-permute-start | bytes 589832 | tf_op jit(solution)/shard_map/ppermute | solution.py:224
  28.1 8.6 %collective-permute-start.4 = (f32[4,16,256]{2,1,0:T(8,128)S(1)}, f32[4,16,256]{2,1,0:T(8,128)S(1)}, u32[]{:S(2)}, u32[]{:S(2)}) collective-permute-start(f32[4,16,256]{2,1,0:T(8,128)S(1)} %pack.1.mine_ref), channel_id=1, source_target_pairs={{0,1},{1,0},{2,3},{3,2},{4,5},{5,4},{6,7},{7,6},{8,9},{9,8},{10,11... | collective-permute-start | bytes 196616 | tf_op jit(solution)/shard_map/ppermute | solution.py:226
